TPU v7x, 32 devices: a whole 2x2x4 slice. The times are simulated.
32 devices in a mesh: chain: 16 (over z, x, core), rep: 2 (over y).
Axes of the slice: x: 2, y: 2, z: 4, core: 2. Of those that a mesh axis runs over, the one named last changes fastest.
Arguments:
- spins: bfloat16 [24576, 256], P('chain'), may hold values from -1 to 1, as said below
- energies: bfloat16 [24576], P('chain'), may hold values from -150 to -70
- counts: int32 [16], P('chain'), may hold values from 1 to 1536, 12288 in all
- accepted: int32 [16, 1536], P('chain'), may hold values from 0 to 1535, each once within a row
- hidden_bias: bfloat16 [4096], P('rep'), may hold values from -3 to 3
- weights: bfloat16 [256, 4096], P(None, 'rep'), may hold values from -0.375 to 0.375
Outputs:
- update_visible: float32 [256], P('rep')
- update_hidden: float32 [4096], P('rep')
- update_weights: float32 [256, 4096], P('chain', 'rep')
Inputs may be any that keep to these rules, and one draw needn't show every extreme that they name: `spins`: every entry is -1 or 1. The counts sum to 12288; at least one index of chain has 1536. Each row is a permutation of the slot numbers; its first counts entries name that index's accepted slots.
All inputs are finite; a program needn't handle non-finite values. No bound on the sum of `counts` on one device may be relied on, other than what follows from the above.
Results may differ from a plain program's by a relative error of at most 0.02.
Values may be sent and summed in bfloat16 or wider, within the bound.
A program may use at most 64 MiB of HBM per device.

v0:
```python
import jax
import jax.numpy as jnp
from jax import lax
from jax.sharding import PartitionSpec as P

N_SITES = 256
HIDDEN_SIZE = 4096
KEEP_DEV = 768
ITERS = 3


PRECISE = lax.Precision.HIGHEST
DIAG_SHIFT = 0.05
EPSILON = 1e-06


def activations(sample_rows, hidden_bias, weights):
    preact = hidden_bias.astype(jnp.float32) + jnp.dot(
        sample_rows, weights, preferred_element_type=jnp.float32
    )
    return jnp.tanh(preact).astype(jnp.bfloat16)


def combine(base_vec, extra_vec, factor):
    return tuple((first + factor * second for first, second in zip(base_vec, extra_vec)))


def per_device(spins, energies, counts, accepted, hidden_bias, weights):
    chain_count = lax.axis_size("chain")
    slot_count = spins.shape[0]
    site_count = spins.shape[1]
    visible_part = site_count // lax.axis_size("rep")
    matrix_rows = site_count // chain_count
    own_count = counts[0]
    accepted_row = accepted[0]
    sample_total = KEEP_DEV * chain_count
    chain_pos = lax.axis_index("chain")
    samples = spins[accepted_row]
    hidden_acts = activations(samples, hidden_bias, weights)
    live_rows = (jnp.arange(slot_count, dtype=jnp.int32) < own_count).astype(jnp.float32)
    energy = energies[accepted_row].astype(jnp.float32)
    visible = lax.dynamic_slice_in_dim(
        samples, lax.axis_index("rep") * visible_part, visible_part, 1
    )
    mean_energy = lax.psum(jnp.sum(energy * live_rows), "chain") / sample_total
    centered = (energy - mean_energy) * live_rows

    def pull(row_weight):
        weighted = hidden_acts.astype(jnp.float32) * row_weight[:, None]
        grad_hid = jnp.sum(weighted, axis=0)
        grad_vis = jnp.dot(
            row_weight, visible, precision=PRECISE, preferred_element_type=jnp.float32
        )
        grad_mat = jnp.einsum(
            "ri,rj->ij", samples, weighted, precision=PRECISE, preferred_element_type=jnp.float32
        )
        grad_vis, grad_hid, grad_mat = lax.psum((grad_vis, grad_hid, grad_mat), "chain")
        return (grad_vis / sample_total, grad_hid / sample_total, grad_mat / sample_total)

    def inner(pairs):
        collected = []
        for first_vec, second_vec in pairs:
            collected.append(
                jnp.sum(first_vec[0] * second_vec[0])
                + jnp.sum(first_vec[1] * second_vec[1])
                + jnp.sum(first_vec[2] * second_vec[2])
            )
        return lax.psum(jnp.stack(collected), "rep")

    force = pull(centered)
    solution = tuple((jnp.zeros_like(member) for member in force))
    residual = force
    direction = force
    resid_sq = inner(((residual, residual),))[0]
    for iteration in range(ITERS):
        vis_part, hid_part, mat_part = direction
        mixture = jnp.dot(samples, mat_part, precision=PRECISE, preferred_element_type=jnp.float32)
        row_values = jnp.sum(mixture * hidden_acts, axis=1)
        row_values = row_values + jnp.dot(
            hidden_acts, hid_part, precision=PRECISE, preferred_element_type=jnp.float32
        )
        row_values = row_values + jnp.dot(
            visible, vis_part, precision=PRECISE, preferred_element_type=jnp.float32
        )
        row_values = lax.psum(row_values, "rep")
        row_mean = lax.psum(jnp.sum(row_values * live_rows), "chain") / sample_total
        image = combine(pull((row_values - row_mean) * live_rows), direction, DIAG_SHIFT)
        products = inner(((direction, image), (residual, image), (image, image)))
        step_size = resid_sq / products[0]
        resid_next = resid_sq - 2.0 * step_size * products[1] + step_size * step_size * products[2]
        solution = combine(solution, direction, step_size)
        residual = combine(residual, image, -step_size)
        if iteration + 1 < ITERS:
            direction = combine(residual, direction, resid_next / resid_sq)
            resid_sq = resid_next
    norm_sq = inner(((solution, solution),))[0]
    param_total = N_SITES * HIDDEN_SIZE + HIDDEN_SIZE + N_SITES
    scale = lax.rsqrt(norm_sq / param_total + EPSILON)
    vis_out = solution[0] * scale
    hid_out = solution[1] * scale
    mat_out = solution[2] * scale
    mat_out = lax.dynamic_slice_in_dim(mat_out, chain_pos * matrix_rows, matrix_rows, 0)
    return (vis_out, hid_out, mat_out)


def solution(mesh):
    in_specs = (
        P("chain", None),
        P("chain"),
        P("chain"),
        P("chain", None),
        P("rep"),
        P(None, "rep"),
    )
    out_specs = (P("rep"), P("rep"), P("chain", "rep"))
    return jax.shard_map(
        per_device, mesh=mesh, in_specs=in_specs, out_specs=out_specs, check_vma=False
    )
```

profile of v0, /device:TPU:0, one launch (start us, length us, event | category | flops | bytes accessed | tf_op | source)
XLA Modules:
  0.0 705.9 jit_solution(17028664585761451023)
XLA Ops:
  8.0 0.7 fusion.26
  8.7 9.5 %gather_fusion = bf16[1536]{0:T(1024)(128)(2,1)S(1)} fusion(bf16[1536]{0:T(1024)(128)(2,1)S(1)} %copy-done.1, s32[2048]{0:T(1024)S(1)} %pad_clamp_fusion), kind=kCustom, calls=%fused_computation | custom fusion | bytes 12288 | tf_op jit(solution)/shard_map/gather | solution.py:41
  18.8 35.5 %psum.168 = f32[]{:T(128)} all-reduce(f32[]{:T(128)} %fusion.24), channel_id=1, replica_groups=mesh['chain'=16,'rep'=2] {'chain'}, use_global_device_ids=true, to_apply=%region_1.0 | all-reduce | flops 1 | bytes 8 | tf_op jit(solution)/shard_map/psum | solution.py:45
  54.3 4.8 gather_fusion.1
  59.8 2.6 fusion.1
  62.4 2.7 copy-done.2
  65.1 8.6 %fusion = f32[256,2048]{1,0:T(8,128)} fusion(bf16[1536,256]{1,0:T(8,128)(2,1)S(1)} %gather_fusion.1, bf16[1536,2048]{1,0:T(8,128)(2,1)S(1)} %get-tuple-element.59, f32[1536]{0:T(1024)S(1)} %fusion.25), kind=kOutput, calls=%fused_computation.9 | convolution fusion | flops 9669967872 | bytes 9181184 | tf_op jit(solution)/shard_map/ri,rj->ij/dot_general | solution.py:54
  74.0 31.6 %all-reduce.3 = (f32[128]{0:T(128)S(1)}, f32[2048]{0:T(1024)S(1)}) all-reduce(f32[128]{0:T(128)S(1)} %convolution_bitcast_fusion.3, f32[2048]{0:T(1024)S(1)} %get-tuple-element.58), channel_id=1, replica_groups=mesh['chain'=16,'rep'=2] {'chain'}, use_global_device_ids=true, to_apply=%region_2.0 | all-reduce | flops 2176 | bytes 17408 | tf_op jit(solution)/shard_map/psum | solution.py:57
  106.1 7.1 %convolution_reduce_fusion.5 = f32[1536]{0:T(1024)S(1)} fusion(bf16[1536,2048]{1,0:T(8,128)(2,1)} %copy-done.2, f32[2048,1]{0,1:T(1,128)S(1)} %bitcast.76), kind=kOutput, calls=%fused_computation.49 | convolution fusion | flops 37748736 | bytes 6305792 | tf_op jit(solution)/shard_map/dot_general | solution.py:79
  113.2 56.4 %all-reduce.10.cloned.1.call-done = f32[256,2048]{1,0:T(8,128)} async-done(((f32[256,2048]{1,0:T(8,128)}), f32[256,2048]{1,0:T(8,128)}) %all-reduce.10.cloned.1.call-update) | async-done | bytes 2097168 | tf_op jit(solution)/shard_map/psum | solution.py:57
  169.7 8.9 %fusion.8 = f32[1536]{0:T(1024)S(1)} fusion(bf16[1536,2048]{1,0:T(8,128)(2,1)} %copy-done.2, bf16[1536,256]{1,0:T(8,128)(2,1)S(1)} %gather_fusion.1, f32[256,2048]{1,0:T(8,128)} %all-reduce.10.cloned.1.call-done), kind=kOutput, calls=%fused_computation.17 | convolution fusion | flops 9673635840 | bytes 9181184 | tf_op jit(solution)/shard_map/dot_general | solution.py:77
  178.6 5.0 psum.173
  184.2 30.1 %psum.174 = f32[]{:T(128)} all-reduce(f32[]{:T(128)} %select_reduce_fusion.2), channel_id=1, replica_groups=mesh['chain'=16,'rep'=2] {'chain'}, use_global_device_ids=true, to_apply=%region_13.0 | all-reduce | flops 1 | bytes 8 | tf_op jit(solution)/shard_map/psum | solution.py:86
  214.9 10.4 %fusion.2 = f32[256,2048]{1,0:T(8,128)} fusion(bf16[1536,256]{1,0:T(8,128)(2,1)S(1)} %gather_fusion.1, bf16[1536,2048]{1,0:T(8,128)(2,1)} %copy-done.2, f32[1536]{0:T(1024)S(1)} %subtract_select_fusion.2), kind=kOutput, calls=%fused_computation.11 | convolution fusion | flops 9669967872 | bytes 9181184 | tf_op jit(solution)/shard_map/ri,rj->ij/dot_general | solution.py:54
  225.7 4.3 fusion.3
  230.0 31.2 %all-reduce.2 = (f32[128]{0:T(128)S(1)}, f32[2048]{0:T(1024)S(1)}) all-reduce(f32[128]{0:T(128)S(1)} %convolution_bitcast_fusion.2, f32[2048]{0:T(1024)S(1)} %fusion.3), channel_id=1, replica_groups=mesh['chain'=16,'rep'=2] {'chain'}, use_global_device_ids=true, to_apply=%region_14.0 | all-reduce | flops 2176 | bytes 17408 | tf_op jit(solution)/shard_map/psum | solution.py:57
  266.4 55.0 %all-reduce.12.cloned.1.call-done = f32[256,2048]{1,0:T(8,128)} async-done(((f32[256,2048]{1,0:T(8,128)}), f32[256,2048]{1,0:T(8,128)}) %all-reduce.12.cloned.1.call-update) | async-done | bytes 2097168 | tf_op jit(solution)/shard_map/psum | solution.py:57
  321.5 3.7 multiply_reduce_fusion.8
  327.2 5.6 all-reduce.4
  337.4 7.2 %convolution_reduce_fusion.3 = f32[1536]{0:T(1024)S(1)} fusion(bf16[1536,2048]{1,0:T(8,128)(2,1)} %copy-done.2, f32[2048,1]{0,1:T(1,128)S(1)} %bitcast.74), kind=kOutput, calls=%fused_computation.47 | convolution fusion | flops 37748736 | bytes 6305792 | tf_op jit(solution)/shard_map/dot_general | solution.py:79
  344.6 2.3 multiply_add_fusion.5
  346.9 6.4 fusion.9
  353.8 5.0 psum.179
  359.4 30.1 %psum.180 = f32[]{:T(128)} all-reduce(f32[]{:T(128)} %select_reduce_fusion.1), channel_id=1, replica_groups=mesh['chain'=16,'rep'=2] {'chain'}, use_global_device_ids=true, to_apply=%region_28.0 | all-reduce | flops 1 | bytes 8 | tf_op jit(solution)/shard_map/psum | solution.py:86
  390.2 10.6 %fusion.4 = f32[256,2048]{1,0:T(8,128)} fusion(bf16[1536,256]{1,0:T(8,128)(2,1)} %copy-done.11, bf16[1536,2048]{1,0:T(8,128)(2,1)} %copy-done.2, f32[1536]{0:T(1024)S(1)} %subtract_select_fusion.1), kind=kOutput, calls=%fused_computation.13 | convolution fusion | flops 9669967872 | bytes 9181184 | tf_op jit(solution)/shard_map/ri,rj->ij/dot_general | solution.py:54
  400.9 1.0 copy-done.13
  402.2 4.4 fusion.5
  406.5 31.6 %all-reduce.1 = (f32[128]{0:T(128)S(1)}, f32[2048]{0:T(1024)S(1)}) all-reduce(f32[128]{0:T(128)S(1)} %convolution_bitcast_fusion.1, f32[2048]{0:T(1024)S(1)} %fusion.5), channel_id=1, replica_groups=mesh['chain'=16,'rep'=2] {'chain'}, use_global_device_ids=true, to_apply=%region_29.0 | all-reduce | flops 2176 | bytes 17408 | tf_op jit(solution)/shard_map/psum | solution.py:57
  438.7 0.7 multiply_reduce_fusion.16
  443.2 53.7 %all-reduce.14.cloned.1.call-done = f32[256,2048]{1,0:T(8,128)} async-done(((f32[256,2048]{1,0:T(8,128)}), f32[256,2048]{1,0:T(8,128)}) %all-reduce.14.cloned.1.call-update) | async-done | bytes 2097168 | tf_op jit(solution)/shard_map/psum | solution.py:57
  496.9 4.4 multiply_reduce_fusion.6
  503.3 4.9 psum.184
  510.9 7.2 %convolution_reduce_fusion.1 = f32[1536]{0:T(1024)S(1)} fusion(bf16[1536,2048]{1,0:T(8,128)(2,1)} %copy-done.2, f32[2048,1]{0,1:T(1,128)S(1)} %bitcast.75), kind=kOutput, calls=%fused_computation.45 | convolution fusion | flops 37748736 | bytes 6305792 | tf_op jit(solution)/shard_map/dot_general | solution.py:79
  518.1 0.8 multiply_add_fusion.2
  519.2 6.4 fusion.10
  526.1 5.0 psum.185
  531.7 30.4 %psum.186 = f32[]{:T(128)} all-reduce(f32[]{:T(128)} %select_reduce_fusion), channel_id=1, replica_groups=mesh['chain'=16,'rep'=2] {'chain'}, use_global_device_ids=true, to_apply=%region_46.0 | all-reduce | flops 1 | bytes 8 | tf_op jit(solution)/shard_map/psum | solution.py:86
  562.8 10.6 %fusion.6 = f32[256,2048]{1,0:T(8,128)} fusion(bf16[1536,256]{1,0:T(8,128)(2,1)} %copy-done.11, bf16[1536,2048]{1,0:T(8,128)(2,1)} %copy-done.2, f32[1536]{0:T(1024)S(1)} %subtract_select_fusion), kind=kOutput, calls=%fused_computation.15 | convolution fusion | flops 9669967872 | bytes 9181184 | tf_op jit(solution)/shard_map/ri,rj->ij/dot_general | solution.py:54
  573.4 1.1 copy-done.15
  574.8 4.5 fusion.7
  579.3 31.3 %all-reduce = (f32[128]{0:T(128)S(1)}, f32[2048]{0:T(1024)S(1)}) all-reduce(f32[128]{0:T(128)S(1)} %convolution_bitcast_fusion, f32[2048]{0:T(1024)S(1)} %fusion.7), channel_id=1, replica_groups=mesh['chain'=16,'rep'=2] {'chain'}, use_global_device_ids=true, to_apply=%region_47.0 | all-reduce | flops 2176 | bytes 17408 | tf_op jit(solution)/shard_map/psum | solution.py:57
  611.2 0.7 multiply_reduce_fusion.13
  615.7 53.8 %all-reduce.16.cloned.1.call-done = f32[256,2048]{1,0:T(8,128)} async-done(((f32[256,2048]{1,0:T(8,128)}), f32[256,2048]{1,0:T(8,128)}) %all-reduce.16.cloned.1.call-update) | async-done | bytes 2097168 | tf_op jit(solution)/shard_map/psum | solution.py:57
  669.5 5.1 multiply_reduce_fusion.3
  676.6 4.9 psum.190
  684.1 4.8 multiply_reduce_fusion
  689.5 6.1 psum.191
  697.4 1.6 dynamic-slice_multiply_fusion
  (93 shorter events, 11.9 us)
Async XLA Ops:
  7.2 52.6 %copy-start = (bf16[256,2048]{1,0:T(8,128)(2,1)S(1)}, bf16[256,2048]{1,0:T(8,128)(2,1)}, u32[]{:S(2)}) copy-start(bf16[256,2048]{1,0:T(8,128)(2,1)} %param.11) | copy-start | bytes 3145732
  7.2 1.5 copy-start.1
  7.2 162.5 %all-reduce.10.cloned.1.call-start = ((), (), s32[]{:S(2)}) async-start(), calls=%async_computation | async-start | bytes 4194304 | tf_op jit(solution)/shard_map/psum | solution.py:57
  8.7 45.6 %copy-start.6 = (bf16[1536,256]{1,0:T(8,128)(2,1)S(1)}, bf16[1536,256]{1,0:T(8,128)(2,1)}, u32[]{:S(2)}) copy-start(bf16[1536,256]{1,0:T(8,128)(2,1)} %param.6) | copy-start | bytes 2359300
  54.3 4.8 copy-start.17
  59.1 166.4 %copy-start.11 = (bf16[1536,256]{1,0:T(8,128)(2,1)}, bf16[1536,256]{1,0:T(8,128)(2,1)S(1)}, u32[]{:S(2)}) copy-start(bf16[1536,256]{1,0:T(8,128)(2,1)S(1)} %gather_fusion.1) | copy-start | bytes 2359300
  62.4 2.7 copy-start.2
  73.7 247.7 %all-reduce.12.cloned.1.call-start = ((), (), s32[]{:S(2)}) async-start(), calls=%async_computation.1 | async-start | bytes 4194304 | tf_op jit(solution)/shard_map/psum | solution.py:57
  225.4 271.5 %all-reduce.14.cloned.1.call-start = ((), (), s32[]{:S(2)}) async-start(), calls=%async_computation.2 | async-start | bytes 4194304 | tf_op jit(solution)/shard_map/psum | solution.py:57
  321.5 25.5 %slice-start = ((s8[6291456]{0:T(1024)(128)(4,1)}), s8[2097152]{0:T(1024)(128)(4,1)S(1)}, s32[]{:S(2)}) async-start(s8[6291456]{0:T(1024)(128)(4,1)} %bitcast.70), calls=%async_computation.4 | async-start | bytes 4194304
  337.4 7.2 %copy-start.8 = (f32[256,2048]{1,0:T(8,128)S(1)}, f32[256,2048]{1,0:T(8,128)}, u32[]{:S(2)}) copy-start(f32[256,2048]{1,0:T(8,128)} %all-reduce.10.cloned.1.call-done) | copy-start | bytes 6291460
  337.4 7.2 %copy-start.16 = (f32[256,2048]{1,0:T(8,128)S(1)}, f32[256,2048]{1,0:T(8,128)}, u32[]{:S(2)}) copy-start(f32[256,2048]{1,0:T(8,128)} %all-reduce.12.cloned.1.call-done) | copy-start | bytes 6291460
  337.4 9.5 %slice-start.1 = ((s8[6291456]{0:T(1024)(128)(4,1)}), s8[4194304]{0:T(1024)(128)(4,1)S(1)}, s32[]{:S(2)}) async-start(s8[6291456]{0:T(1024)(128)(4,1)} %bitcast.70), calls=%async_computation.5 | async-start | bytes 8388608
  344.6 2.3 copy-start.12
  346.9 6.4 copy-start.3
  400.8 1.1 copy-start.13
  400.8 268.6 %all-reduce.16.cloned.1.call-start = ((), (), s32[]{:S(2)}) async-start(), calls=%async_computation.3 | async-start | bytes 4194304 | tf_op jit(solution)/shard_map/psum | solution.py:57
  496.9 22.1 %slice-start.2 = ((s8[6291456]{0:T(1024)(128)(4,1)}), s8[2097152]{0:T(1024)(128)(4,1)S(1)}, s32[]{:S(2)}) async-start(s8[6291456]{0:T(1024)(128)(4,1)} %bitcast.72), calls=%async_computation.6 | async-start | bytes 4194304
  510.9 7.2 %copy-start.4 = (f32[256,2048]{1,0:T(8,128)S(1)}, f32[256,2048]{1,0:T(8,128)}, u32[]{:S(2)}) copy-start(f32[256,2048]{1,0:T(8,128)} %copy-done.3) | copy-start | bytes 6291460
  510.9 7.2 %copy-start.7 = (f32[256,2048]{1,0:T(8,128)S(1)}, f32[256,2048]{1,0:T(8,128)}, u32[]{:S(2)}) copy-start(f32[256,2048]{1,0:T(8,128)} %get-tuple-element.49) | copy-start | bytes 6291460
  510.9 7.2 %copy-start.10 = (f32[256,2048]{1,0:T(8,128)S(1)}, f32[256,2048]{1,0:T(8,128)}, u32[]{:S(2)}) copy-start(f32[256,2048]{1,0:T(8,128)} %all-reduce.14.cloned.1.call-done) | copy-start | bytes 6291460
  510.9 8.1 %slice-start.3 = ((s8[6291456]{0:T(1024)(128)(4,1)}), s8[4194304]{0:T(1024)(128)(4,1)S(1)}, s32[]{:S(2)}) async-start(s8[6291456]{0:T(1024)(128)(4,1)} %bitcast.72), calls=%async_computation.7 | async-start | bytes 8388608
  518.1 1.1 copy-start.14
  519.2 6.4 copy-start.9
  573.4 1.1 copy-start.15
  574.8 94.7 %copy-start.5 = (f32[256,2048]{1,0:T(8,128)S(1)}, f32[256,2048]{1,0:T(8,128)}, u32[]{:S(2)}) copy-start(f32[256,2048]{1,0:T(8,128)} %copy-done.3) | copy-start | bytes 6291460
Sparse Core Ops, SparseCore 0:
  73.8 95.7 all-reduce.9
  225.5 95.9 all-reduce.11
  400.9 95.9 all-reduce.13
  573.5 95.8 all-reduce.15
where the time goes:
time: 714 us; the launch traced here: 706 us
  blocking collectives  288 us (40%)
  waiting for transfers between devices  219 us (31%)
  matrix products  88.2 us (12%)
  other arithmetic  45.5 us (6%)
  between operations  44.1 us (6%)
  local copies, waits for them, and re-layouts  20.7 us (3%)
    psum x4, waiting for transfers between devices, pull(): lax.psum((grad_vis, grad_hid, grad_mat), 'chain')  219 us
    psum x4, blocking collectives, pull(): lax.psum((grad_vis, grad_hid, grad_mat), 'chain')  126 us
    psum x3, blocking collectives, per_device(): row_mean = lax.psum(jnp.sum(row_values * live_rows), 'chain') / sample_total  90.6 us
    dot_general x4, matrix products, pull(): jnp.einsum('ri,rj->ij', samples, weighted, precision=PRECISE, preferred_e...  40.2 us
    psum x1, blocking collectives, per_device(): mean_energy = lax.psum(jnp.sum(energy * live_rows), 'chain') / sample_total  35.5 us
    dot_general x3, matrix products, per_device(): jnp.dot(samples, mat_part, precision=PRECISE, preferred_element_type=jnp....  21.7 us
    psum x4, blocking collectives, inner(): return lax.psum(jnp.stack(collected), 'rep')  21.5 us
    dot_general x3, matrix products, per_device(): jnp.dot(hidden_acts, hid_part, precision=PRECISE, preferred_element_type=...  21.4 us
  transfers between devices with their start and end apart: 4, of which 4 were waited for; matrix products, arithmetic and copies ran while one was open for 4% of the time, Pallas kernels for 0%

commit v1 on v0

v1 whole, which is shorter than its diff:
```python
import jax
import jax.numpy as jnp
from jax import lax
from jax.sharding import PartitionSpec as P

N_SITES = 256
HIDDEN_SIZE = 4096
KEEP_DEV = 768
ITERS = 3

DIAG_SHIFT = 0.05
EPSILON = 1e-06


def per_device(spins, energies, counts, accepted, hidden_bias, weights):
    chain_count = lax.axis_size("chain")
    slot_count, site_count = spins.shape
    hidden_part = weights.shape[1]
    visible_part = site_count // lax.axis_size("rep")
    matrix_rows = site_count // chain_count
    sample_total = KEEP_DEV * chain_count
    chain_pos = lax.axis_index("chain")
    rep_pos = lax.axis_index("rep")
    f32 = jnp.float32

    slots = jnp.arange(slot_count, dtype=jnp.int32)
    names = jnp.where(slots < counts[0], accepted[0], -1)
    live = jnp.sum((slots[:, None] == names[None, :]).astype(f32), axis=1)
    energy = energies.astype(f32) * live
    mean_energy = lax.psum(jnp.sum(energy), "chain") / sample_total
    centered = energy - mean_energy * live

    preact = hidden_bias.astype(f32) + jnp.dot(spins, weights, preferred_element_type=f32)
    acts = jnp.tanh(preact).astype(jnp.bfloat16)
    visible = lax.dynamic_slice_in_dim(spins, rep_pos * visible_part, visible_part, 1)

    def pull(row_weight):
        weighted = acts.astype(f32) * row_weight[:, None]
        mat = lax.dot_general(
            spins,
            weighted.astype(jnp.bfloat16),
            (((0,), (0,)), ((), ())),
            preferred_element_type=f32,
        )
        hid = jnp.sum(weighted, axis=0)
        vis = jnp.sum(visible.astype(f32) * row_weight[:, None], axis=0)
        mat = lax.psum((mat / sample_total).astype(jnp.bfloat16), "chain")
        vec = lax.psum(jnp.concatenate([hid, vis]) / sample_total, "chain")
        return (mat, vec[:hidden_part], vec[hidden_part:])

    def push(parts):
        mat, hid, vis = parts
        mixture = jnp.dot(spins, mat, preferred_element_type=f32) + hid
        row_values = jnp.sum(mixture * acts.astype(f32), axis=1)
        row_values = row_values + jnp.sum(visible.astype(f32) * vis, axis=1)
        return lax.psum(row_values, "rep") * live

    def sums(*pairs):
        return lax.psum(jnp.stack([jnp.sum(a * b) for a, b in pairs]), "chain")

    def mix(one, other, factor):
        return tuple(a + factor * b for a, b in zip(one, other))

    base = [pull(centered)]
    image_raw = push(base[0])
    total, = sums((image_raw, live))
    image0 = image_raw - live * (total / sample_total)
    unit = [jnp.array([1.0 if i == j else 0.0 for j in range(ITERS)], f32) for i in range(ITERS)]
    direction = (centered, image0, unit[0])
    residual = direction
    answer = tuple(jnp.zeros_like(a) for a in direction)
    resid_sq = None
    for iteration in range(ITERS):
        dd, dc, rc = sums((direction[1], direction[1]), (direction[1], direction[0]), (residual[1], residual[0]))
        if iteration == 0:
            resid_sq = rc
        step = resid_sq / (dd + DIAG_SHIFT * dc)
        answer = mix(answer, direction, step)
        if iteration + 1 == ITERS:
            break
        base.append(pull(direction[1]))
        raw = push(base[-1])
        total, = sums((raw, live))
        applied = (direction[1], raw - live * (total / sample_total), unit[iteration + 1])
        residual = mix(residual, mix(applied, direction, DIAG_SHIFT), -step)
        resid_next, = sums((residual[1], residual[0]))
        direction = mix(residual, direction, resid_next / resid_sq)
        resid_sq = resid_next
    norm_sq, = sums((answer[1], answer[0]))
    norm_sq = norm_sq / sample_total
    param_total = N_SITES * HIDDEN_SIZE + HIDDEN_SIZE + N_SITES
    scale = lax.rsqrt(norm_sq / param_total + EPSILON)
    pick = answer[2] * scale
    mat_out = 0.0
    hid_out = 0.0
    vis_out = 0.0
    for k, (mat, hid, vis) in enumerate(base):
        own = lax.dynamic_slice_in_dim(mat, chain_pos * matrix_rows, matrix_rows, 0)
        mat_out = mat_out + pick[k] * own.astype(f32)
        hid_out = hid_out + pick[k] * hid
        vis_out = vis_out + pick[k] * vis
    return (vis_out, hid_out, mat_out)


def solution(mesh):
    in_specs = (
        P("chain", None),
        P("chain"),
        P("chain"),
        P("chain", None),
        P("rep"),
        P(None, "rep"),
    )
    out_specs = (P("rep"), P("rep"), P("chain", "rep"))
    return jax.shard_map(
        per_device, mesh=mesh, in_specs=in_specs, out_specs=out_specs, check_vma=False
    )
```

time: 714 us -> 624 us (0.87)
  blocking collectives: 288 us -> 435 us
  waiting for transfers between devices: 219 us -> 86.3 us
  matrix products: 88.2 us -> 35 us
  between operations: 44.1 us -> 26 us
  local copies, waits for them, and re-layouts: 20.7 us -> 6.19 us
  other arithmetic: 45.5 us -> 34.3 us
    psum x15 -> x14, blocking collectives: 288 us -> 435 us  [the longest x7 210 us: sums(): return lax.psum(jnp.stack([jnp.sum(a * b) for a, b in pairs]), 'chain')]
    psum x4 -> x3, waiting for transfers between devices: 219 us -> 86.3 us  [pull(): mat = lax.psum((mat / sample_total).astype(jnp.bfloat16), 'chain')]
    dot_general x18 -> x7, matrix products: 88.2 us -> 35 us  [the longest x3 16 us: pull(): lax.dot_general(spins, weighted.astype(jnp.bfloat16), (((0,), (0,)), ((),...]
    reduce_sum x19, other arithmetic: 38.6 us -> 18 us  [the longest x2 8.23 us: pull(): hid = jnp.sum(weighted, axis=0)]
    gather x2 -> x0, local copies, waits for them, and re-layouts: 14.2 us -> none  [the longest x1 9.46 us: per_device(): energy = energies[accepted_row].astype(jnp.float32)]
  transfers between devices with their start and end apart: 4 -> 3, of which waited for: 4 -> 3; matrix products, arithmetic and copies ran while one was open for 4% -> 2% of each run, Pallas kernels for 0% -> 0%
where the time goes in v1:
time: 624 us; the launch traced here: 623 us
  blocking collectives  435 us (70%)
  waiting for transfers between devices  86.3 us (14%)
  matrix products  35 us (6%)
  other arithmetic  34.3 us (5%)
  between operations  26 us (4%)
    psum x7, blocking collectives, sums(): return lax.psum(jnp.stack([jnp.sum(a * b) for a, b in pairs]), 'chain')  210 us
    psum x3, blocking collectives, pull(): vec = lax.psum(jnp.concatenate([hid, vis]) / sample_total, 'chain')  174 us
    psum x3, waiting for transfers between devices, pull(): mat = lax.psum((mat / sample_total).astype(jnp.bfloat16), 'chain')  86.3 us
    psum x1, blocking collectives, per_device(): mean_energy = lax.psum(jnp.sum(energy), 'chain') / sample_total  35.5 us
    dot_general x3, matrix products, pull(): lax.dot_general(spins, weighted.astype(jnp.bfloat16), (((0,), (0,)), ((),...  16 us
    dot_general x3, matrix products, push(): mixture = jnp.dot(spins, mat, preferred_element_type=f32) + hid  15.5 us
    psum x3, blocking collectives, push(): return lax.psum(row_values, 'rep') * live  15 us
  transfers between devices with their start and end apart: 3, of which 3 were waited for; matrix products, arithmetic and copies ran while one was open for 2% of the time, Pallas kernels for 0%

profile of v1, /device:TPU:0, one launch (start us, length us, event | category | flops | bytes accessed | tf_op | source)
XLA Modules:
  0.0 622.7 jit_solution(10950135379604152361)
XLA Ops:
  8.0 0.7 fusion.52
  8.7 1.0 convert_reduce_fusion
  9.7 1.3 fusion.51
  11.0 35.5 %psum.133 = f32[]{:T(128)} all-reduce(f32[]{:T(128)} %fusion.51), channel_id=1, replica_groups=mesh['chain'=16,'rep'=2] {'chain'}, use_global_device_ids=true, to_apply=%region_2.3 | all-reduce | flops 1 | bytes 8 | tf_op jit(solution)/shard_map/psum | solution.py:30
  47.2 0.7 multiply_subtract_fusion.1
  47.9 0.7 convert_element_type.64
  48.6 3.5 fusion
  52.1 2.7 copy-done.1
  54.8 3.6 fusion.36
  58.8 58.0 %psum.135 = f32[2176]{0:T(1024)S(1)} all-reduce(f32[2176]{0:T(1024)S(1)} %maximum_multiply_fusion), channel_id=1, replica_groups=mesh['chain'=16,'rep'=2] {'chain'}, use_global_device_ids=true, to_apply=%region_6.7 | all-reduce | flops 2176 | bytes 17408 | tf_op jit(solution)/shard_map/psum | solution.py:48
  117.1 32.5 %all-reduce.6.cloned.1.call-done = bf16[256,2048]{0,1:T(8,128)(2,1)} async-done(((bf16[256,2048]{0,1:T(8,128)(2,1)}), bf16[256,2048]{0,1:T(8,128)(2,1)}) %all-reduce.6.cloned.1.call-update) | async-done | bytes 1048592 | tf_op jit(solution)/shard_map/psum | solution.py:47
  149.6 5.2 fusion.6
  154.8 5.0 psum.136
  160.4 30.1 %psum.137 = f32[1]{0:T(128)} all-reduce(f32[1]{0:T(128)} %bitcast.3), channel_id=1, replica_groups=mesh['chain'=16,'rep'=2] {'chain'}, use_global_device_ids=true, to_apply=%region_11.12 | all-reduce | flops 1 | bytes 8 | tf_op jit(solution)/shard_map/psum | solution.py:59
  191.1 0.6 multiply_reduce_fusion.10
  191.7 6.2 %fusion.39 = bf16[256,2048]{0,1:T(8,128)(2,1)} fusion(bf16[1536,256]{1,0:T(8,128)(2,1)S(1)} %copy-done.2, bf16[1536,2048]{1,0:T(8,128)(2,1)} %copy-done.1, f32[1536]{0:T(1024)S(1)} %get-tuple-element.26), kind=kOutput, calls=%fused_computation.31 | convolution fusion | flops 1621098496 | bytes 8132608 | tf_op jit(solution)/shard_map/dot_general | solution.py:39
  198.2 4.2 fusion.2
  202.7 57.9 %psum.140 = f32[2176]{0:T(1024)S(1)} all-reduce(f32[2176]{0:T(1024)S(1)} %maximum_multiply_fusion.1), channel_id=1, replica_groups=mesh['chain'=16,'rep'=2] {'chain'}, use_global_device_ids=true, to_apply=%region_18.19 | all-reduce | flops 2176 | bytes 17408 | tf_op jit(solution)/shard_map/psum | solution.py:48
  260.6 1.4 pad_maximum_fusion
  262.2 27.1 %all-reduce.8.cloned.1.call-done = bf16[256,2048]{0,1:T(8,128)(2,1)} async-done(((bf16[256,2048]{0,1:T(8,128)(2,1)}), bf16[256,2048]{0,1:T(8,128)(2,1)}) %all-reduce.8.cloned.1.call-update) | async-done | bytes 1048592 | tf_op jit(solution)/shard_map/psum | solution.py:47
  289.4 5.2 fusion.7
  294.5 5.0 psum.141
  300.2 30.1 %all-reduce.1 = (f32[3]{0:T(128)S(1)}, f32[1]{0:T(128)}) all-reduce(f32[3]{0:T(128)S(1)} %pad_maximum_fusion, f32[1]{0:T(128)} %bitcast.10), channel_id=1, replica_groups=mesh['chain'=16,'rep'=2] {'chain'}, use_global_device_ids=true, to_apply=%region_14.15 | all-reduce | flops 4 | bytes 32 | tf_op jit(solution)/shard_map/psum | solution.py:59
  333.4 0.6 multiply_reduce_fusion.7
  334.0 30.1 %psum.143 = f32[1]{0:T(128)} all-reduce(f32[1]{0:T(128)} %bitcast.12), channel_id=1, replica_groups=mesh['chain'=16,'rep'=2] {'chain'}, use_global_device_ids=true, to_apply=%region_25.26 | all-reduce | flops 1 | bytes 8 | tf_op jit(solution)/shard_map/psum | solution.py:59
  365.2 0.7 multiply_reduce_fusion.6
  365.9 6.1 fusion.42
  372.0 4.1 fusion.4
  376.4 58.0 %psum.146 = f32[2176]{0:T(1024)S(1)} all-reduce(f32[2176]{0:T(1024)S(1)} %maximum_multiply_fusion.2), channel_id=1, replica_groups=mesh['chain'=16,'rep'=2] {'chain'}, use_global_device_ids=true, to_apply=%region_32.33 | all-reduce | flops 2176 | bytes 17408 | tf_op jit(solution)/shard_map/psum | solution.py:48
  434.4 2.0 pad_maximum_fusion.1
  436.7 26.6 %all-reduce.10.cloned.1.call-done = bf16[256,2048]{0,1:T(8,128)(2,1)} async-done(((bf16[256,2048]{0,1:T(8,128)(2,1)}), bf16[256,2048]{0,1:T(8,128)(2,1)}) %all-reduce.10.cloned.1.call-update) | async-done | bytes 1048592 | tf_op jit(solution)/shard_map/psum | solution.py:47
  463.3 5.2 fusion.8
  468.5 5.0 psum.147
  474.1 30.1 %all-reduce = (f32[1]{0:T(128)}, f32[3]{0:T(128)S(1)}) all-reduce(f32[1]{0:T(128)} %bitcast.19, f32[3]{0:T(128)S(1)} %pad_maximum_fusion.1), channel_id=1, replica_groups=mesh['chain'=16,'rep'=2] {'chain'}, use_global_device_ids=true, to_apply=%region_37.38 | all-reduce | flops 4 | bytes 32 | tf_op jit(solution)/shard_map/psum | solution.py:59
  504.2 0.6 fusion.57
  507.4 0.7 multiply_reduce_fusion.3
  508.0 30.1 %psum.149 = f32[1]{0:T(128)} all-reduce(f32[1]{0:T(128)} %bitcast.21), channel_id=1, replica_groups=mesh['chain'=16,'rep'=2] {'chain'}, use_global_device_ids=true, to_apply=%region_39.40 | all-reduce | flops 1 | bytes 8 | tf_op jit(solution)/shard_map/psum | solution.py:59
  539.4 0.7 multiply_reduce_fusion.2
  540.1 2.1 pad_maximum_fusion.2
  542.1 29.5 %psum.150 = f32[3]{0:T(128)S(1)} all-reduce(f32[3]{0:T(128)S(1)} %pad_maximum_fusion.2), channel_id=1, replica_groups=mesh['chain'=16,'rep'=2] {'chain'}, use_global_device_ids=true, to_apply=%region_42.43 | all-reduce | flops 3 | bytes 24 | tf_op jit(solution)/shard_map/psum | solution.py:59
  571.6 0.7 fusion.56
  574.2 0.7 multiply_reduce_fusion
  574.9 30.2 %psum.151 = f32[1]{0:T(128)} all-reduce(f32[1]{0:T(128)} %bitcast.26), channel_id=1, replica_groups=mesh['chain'=16,'rep'=2] {'chain'}, use_global_device_ids=true, to_apply=%region_44.45 | all-reduce | flops 1 | bytes 8 | tf_op jit(solution)/shard_map/psum | solution.py:59
  605.8 0.7 fusion.55
  606.5 2.4 multiply_add_fusion.10
  608.9 2.5 multiply_add_fusion.1
  611.4 3.8 multiply_add_fusion
  615.2 1.0 copy.19
  (40 shorter events, 4.5 us)
Async XLA Ops:
  7.2 41.4 %copy-start = (bf16[256,2048]{1,0:T(8,128)(2,1)S(1)}, bf16[256,2048]{1,0:T(8,128)(2,1)}, u32[]{:S(2)}) copy-start(bf16[256,2048]{1,0:T(8,128)(2,1)} %param.14) | copy-start | bytes 3145732
  7.2 142.4 %all-reduce.6.cloned.1.call-start = ((), (), s32[]{:S(2)}) async-start(), calls=%async_computation | async-start | bytes 2097152 | tf_op jit(solution)/shard_map/psum | solution.py:47
  48.6 6.2 copy-start.2
  52.1 2.7 copy-start.1
  58.4 230.9 %all-reduce.8.cloned.1.call-start = ((), (), s32[]{:S(2)}) async-start(), calls=%async_computation.1 | async-start | bytes 2097152 | tf_op jit(solution)/shard_map/psum | solution.py:47
  198.0 265.3 %all-reduce.10.cloned.1.call-start = ((), (), s32[]{:S(2)}) async-start(), calls=%async_computation.2 | async-start | bytes 2097152 | tf_op jit(solution)/shard_map/psum | solution.py:47
  436.7 169.1 %copy-start.3 = (f32[3]{0:T(128)S(1)}, f32[3]{0:T(128)}, u32[]{:S(2)}) copy-start(f32[3]{0:T(128)} %constant.63.clone) | copy-start | bytes 40
  436.7 169.1 %copy-start.4 = (f32[3]{0:T(128)S(1)}, f32[3]{0:T(128)}, u32[]{:S(2)}) copy-start(f32[3]{0:T(128)} %constant.61.clone) | copy-start | bytes 40
  436.7 169.1 %copy-start.5 = (f32[3]{0:T(128)S(1)}, f32[3]{0:T(128)}, u32[]{:S(2)}) copy-start(f32[3]{0:T(128)} %constant.67) | copy-start | bytes 40
Sparse Core Ops, SparseCore 0:
  58.5 90.9 all-reduce.5
  198.1 91.2 all-reduce.7
  372.2 91.1 all-reduce.9

commit v2 on v0

v2 whole, which is shorter than its diff:
```python
import functools

import jax
import jax.numpy as jnp
from jax import lax
from jax.experimental import pallas as pl
from jax.experimental.pallas import tpu as pltpu
from jax.sharding import PartitionSpec as P

N_SITES = 256
HIDDEN_SIZE = 4096
KEEP_DEV = 768
ITERS = 3

DIAG_SHIFT = 0.05
EPSILON = 1e-06
LANES = 128
MIN_ROWS = 16
MESH = pl.DeviceIdType.MESH
F32 = jnp.float32
BF16 = jnp.bfloat16


def to_row(column):
    return jnp.transpose(jnp.broadcast_to(column, (LANES, LANES)))[:1, :]


def to_column(row):
    return jnp.transpose(jnp.broadcast_to(row, (LANES, LANES)))[:, :1]


def total(values):
    return jnp.sum(values, axis=1, keepdims=True)


def kernel(
    n_chain, n_rep, s_ref, st_ref, wt_ref, bias_ref, energy_ref, live_ref,
    mat_ref, vec_ref, acts, acc, outbox, inbox, pulled, vecs, vec_in, rowsum, rows, gathered,
    mat_send, mat_recv, back_send, back_recv, vec_send, vec_recv, row_send, row_recv,
    tell_send, tell_recv,
):
    slots, sites = s_ref.shape
    hidden = wt_ref.shape[0]
    visible = sites // n_rep
    sample_total = float(KEEP_DEV * n_chain)
    bits = n_chain.bit_length() - 1
    tile = min(256, hidden // 2)
    chunks = tile // LANES
    vis_row = hidden // LANES
    me = lax.axis_index("chain")
    rep = lax.axis_index("rep")
    lane = lax.broadcasted_iota(jnp.int32, (1, LANES), 1)

    barrier = pltpu.get_barrier_semaphore()

    @pl.loop(1, n_chain)
    def _(k):
        pl.semaphore_signal(
            barrier, inc=1, device_id={"chain": lax.rem(me + k, n_chain)}, device_id_type=MESH
        )

    for k in range(1, n_rep):
        pl.semaphore_signal(
            barrier, inc=1, device_id={"rep": lax.rem(rep + k, n_rep)}, device_id_type=MESH
        )
    pl.semaphore_wait(barrier, n_chain - 1 + n_rep - 1)

    def tell_copy(sync, source, target):
        return pltpu.make_async_remote_copy(
            src_ref=gathered.at[sync, source],
            dst_ref=gathered.at[sync, source],
            send_sem=tell_send.at[sync, target],
            recv_sem=tell_recv.at[sync, source],
            device_id={"chain": target},
            device_id_type=MESH,
        )

    def tell(sync, values):
        packed = jnp.zeros((1, LANES), F32)
        for j, value in enumerate(values):
            packed = jnp.where(lane == j, value, packed)
        weight = jnp.broadcast_to(values[0], (1, LANES))
        middle = jnp.broadcast_to(values[1], (1, LANES))
        blank = jnp.zeros((5, LANES), F32)
        gathered[sync, me] = jnp.concatenate([packed, weight, middle, blank], axis=0)

        @pl.loop(1, n_chain)
        def _(k):
            tell_copy(sync, me, lax.rem(me + k, n_chain)).start()

    def hear(sync, count):
        @pl.loop(1, n_chain)
        def _(k):
            tell_copy(sync, lax.rem(me + k, n_chain), lax.rem(me + k, n_chain)).wait_recv()

        @pl.loop(1, n_chain)
        def _(k):
            tell_copy(sync, me, lax.rem(me + k, n_chain)).wait_send()

        everyone = [gathered[sync, j] for j in range(n_chain)]
        packed = everyone[0][0:1]
        weighted = everyone[0][1:2] * everyone[0][2:3]
        for one in everyone[1:]:
            packed = packed + one[0:1]
            weighted = weighted + one[1:2] * one[2:3]
        mean = weighted / sample_total
        spread = jnp.zeros((1, LANES), F32)
        for one in everyone:
            spread = spread + one[1:2] * (one[2:3] - mean) * (one[2:3] - mean)
        found = [total(jnp.where(lane == j, packed, 0.0)) for j in range(count)]
        return mean[:, :1], spread[:, :1], found

    vecs[...] = jnp.zeros_like(vecs)
    live = live_ref[...]
    own_count = total(live)
    energy = energy_ref[...]
    tell(0, [own_count, total(energy * live) / own_count])

    @pl.loop(0, hidden // tile)
    def _(i):
        part = pl.ds(pl.multiple_of(i * tile, tile), tile)
        preact = jnp.dot(wt_ref[part, :], st_ref[...], preferred_element_type=F32)
        bias = [to_column(bias_ref[pl.ds(i * chunks + r, 1), :]) for r in range(chunks)]
        acts[part, :] = jnp.tanh(preact + jnp.concatenate(bias, axis=0)).astype(BF16)

    mean_energy, _, _ = hear(0, 0)
    centered = (energy - mean_energy) * live

    own_visible = pl.ds(pl.multiple_of(rep * visible, visible), visible)

    def pull_tiles(k, first, count, row_weight):
        @pl.loop(0, count)
        def _(i):
            begin = first + i * tile
            part = pl.ds(pl.multiple_of(begin, tile), tile)
            weighted = acts[part, :].astype(F32) * row_weight
            sums = jnp.sum(weighted, axis=1, keepdims=True)
            for r in range(chunks):
                row = to_row(sums[r * LANES : (r + 1) * LANES])
                vecs[k, pl.ds(begin // LANES + r, 1), :] = row
            acc[part, :] = jnp.dot(
                weighted.astype(BF16), s_ref[...], preferred_element_type=F32
            )

    def peer(b):
        digit = lax.rem(me // (2**b), 2)
        return digit, me + (1 - 2 * digit) * (2**b)

    def push_tiles(k, first, count):
        @pl.loop(0, count)
        def _(i):
            begin = first + i * tile
            part = pl.ds(pl.multiple_of(begin, tile), tile)
            mixture = jnp.dot(pulled[k, part, :], st_ref[...], preferred_element_type=F32)
            shift = [to_column(vecs[k, pl.ds(begin // LANES + r, 1), :]) for r in range(chunks)]
            mixture = mixture + jnp.concatenate(shift, axis=0)
            product = mixture * acts[part, :].astype(F32)
            rowsum[...] += jnp.sum(product.reshape(tile // 8, 8, slots), axis=0)

    def apply(k, row_weight):
        row_weight = row_weight / sample_total
        sums = jnp.sum(st_ref[own_visible, :].astype(F32) * row_weight, axis=1, keepdims=True)
        if visible < LANES:
            sums = jnp.concatenate([sums, jnp.zeros((LANES - visible, 1), F32)], axis=0)
        vecs[k, vis_row : vis_row + 1, :] = to_row(sums)

        start, size, place = 0, hidden, 0
        steps = []
        for b in range(bits):
            digit, partner = peer(b)
            split = size // 2 >= MIN_ROWS
            moved = size // 2 if split else size
            away = start + (1 - digit) * moved if split else start
            keep = start + digit * moved if split else start
            away = pl.multiple_of(away, moved)
            keep = pl.multiple_of(keep, moved)
            if b == 0:
                pull_tiles(k, away, moved // tile, row_weight)
            outbox[pl.ds(place, moved), :] = acc[pl.ds(away, moved), :].astype(BF16)
            send = pltpu.make_async_remote_copy(
                src_ref=outbox.at[pl.ds(place, moved)],
                dst_ref=inbox.at[pl.ds(place, moved)],
                send_sem=mat_send.at[k, b],
                recv_sem=mat_recv.at[k, b],
                device_id={"chain": partner},
                device_id_type=MESH,
            )
            send.start()
            if b == 0:
                pull_tiles(k, keep, moved // tile, row_weight)
            spread = pltpu.make_async_remote_copy(
                src_ref=vecs.at[k],
                dst_ref=vec_in.at[k, b],
                send_sem=vec_send.at[k, b],
                recv_sem=vec_recv.at[k, b],
                device_id={"chain": partner},
                device_id_type=MESH,
            )
            spread.start()
            send.wait()
            own = acc[pl.ds(keep, moved), :]
            if not split:
                own = own.astype(BF16).astype(F32)
            acc[pl.ds(keep, moved), :] = own + inbox[pl.ds(place, moved), :].astype(F32)
            spread.wait()
            vecs[k] = vecs[k] + vec_in[k, b]
            place += moved
            start, size = keep, moved
            steps.append((b, partner, split, keep, moved))
        pulled[k, pl.ds(start, size), :] = acc[pl.ds(start, size), :].astype(BF16)
        rowsum[...] = jnp.zeros_like(rowsum)
        for b, partner, split, keep, moved in reversed(steps):
            if not split:
                continue
            part = pl.ds(pl.multiple_of(keep, moved), moved)
            send = pltpu.make_async_remote_copy(
                src_ref=pulled.at[k, part],
                dst_ref=pulled.at[k, part],
                send_sem=back_send.at[k, b],
                recv_sem=back_recv.at[k, b],
                device_id={"chain": partner},
                device_id_type=MESH,
            )
            send.start()
            if b == 0:
                push_tiles(k, keep, moved // tile)
            send.wait()
            if b == 0:
                push_tiles(k, hidden - moved - keep, moved // tile)
        seen = jnp.sum(rowsum[...], axis=0, keepdims=True)
        effect = to_column(vecs[k, vis_row : vis_row + 1, :])[:visible]
        seen = seen + jnp.sum(st_ref[own_visible, :].astype(F32) * effect, axis=0, keepdims=True)
        rows[k, rep, 0:1, :] = seen

        def row_copy(source, target):
            return pltpu.make_async_remote_copy(
                src_ref=rows.at[k, source, pl.ds(0, 1)],
                dst_ref=rows.at[k, source, pl.ds(0, 1)],
                send_sem=row_send.at[k, target],
                recv_sem=row_recv.at[k, source],
                device_id={"rep": target},
                device_id_type=MESH,
            )

        others = [lax.rem(rep + d, n_rep) for d in range(1, n_rep)]
        for other in others:
            row_copy(rep, other).start()
        for other in others:
            row_copy(other, other).wait_recv()
        for other in others:
            row_copy(rep, other).wait_send()
        whole = rows[k, 0, 0:1, :]
        for j in range(1, n_rep):
            whole = whole + rows[k, j, 0:1, :]
        return whole * live

    raw = apply(0, centered)
    middle = total(raw) / own_count
    local = (raw - middle) * live
    tell(1, [own_count, middle, total(local * local), total(raw * centered)])
    mean, spread, found = hear(1, 4)
    image = (raw - mean) * live
    dir_dir = found[2] + spread
    dir_wgt = found[3]
    resid_sq = dir_wgt
    dir_w, dir_o, dir_c = centered, image, [1.0, 0.0, 0.0]
    res_w, res_o, res_c = centered, image, [1.0, 0.0, 0.0]
    step = resid_sq / (dir_dir + DIAG_SHIFT * dir_wgt)
    ans_w, ans_o = step * dir_w, step * dir_o
    ans_c = [step * x for x in dir_c]
    norm = None
    for i in range(1, ITERS):
        raw = apply(i, dir_o)
        unit = [1.0 if j == i else 0.0 for j in range(ITERS)]
        res_w = res_w - step * (dir_o + DIAG_SHIFT * dir_w)
        res_c = [r - step * (u + DIAG_SHIFT * d) for r, u, d in zip(res_c, unit, dir_c)]
        fresh = res_o - step * (raw + DIAG_SHIFT * dir_o)
        middle = total(fresh * live) / own_count
        local = (fresh - middle) * live
        tell(i + 1, [
            own_count, middle, total(local * local), total(fresh * dir_o), total(fresh * res_w),
            total(fresh * dir_w), total(dir_o * res_w), total(fresh * ans_w),
            total(dir_o * ans_w), total(ans_o * ans_w),
        ])
        mean, spread, found = hear(i + 1, 10)
        res_o = (fresh - mean) * live
        _, _, res_res, res_dir, resid_next, res_dirw, dir_resw, res_ans, dir_ans, ans_ans = found
        res_res = res_res + spread
        ratio = resid_next / resid_sq
        new_dir = res_res + 2.0 * ratio * res_dir + ratio * ratio * dir_dir
        new_wgt = resid_next + ratio * (res_dirw + dir_resw) + ratio * ratio * dir_wgt
        mixed = res_ans + ratio * dir_ans
        dir_w = res_w + ratio * dir_w
        dir_o = res_o + ratio * dir_o
        dir_c = [r + ratio * d for r, d in zip(res_c, dir_c)]
        dir_dir, dir_wgt, resid_sq = new_dir, new_wgt, resid_next
        step = resid_sq / (dir_dir + DIAG_SHIFT * dir_wgt)
        norm = (ans_ans + 2.0 * step * mixed + step * step * dir_wgt) / sample_total
        ans_w, ans_o = ans_w + step * dir_w, ans_o + step * dir_o
        ans_c = [a + step * d for a, d in zip(ans_c, dir_c)]
    params = N_SITES * HIDDEN_SIZE + HIDDEN_SIZE + N_SITES
    scale = lax.rsqrt(norm / params + EPSILON)
    own_rows = mat_ref.shape[0]
    picks = lax.broadcasted_iota(jnp.int32, (MIN_ROWS, sites), 0) + me * own_rows
    picks = (picks == lax.broadcasted_iota(jnp.int32, (MIN_ROWS, sites), 1)).astype(BF16)
    for i in range(hidden // tile):
        part = slice(i * tile, (i + 1) * tile)
        out = 0.0
        for k in range(ITERS):
            piece = lax.dot_general(
                picks, pulled[k, part, :], (((1,), (1,)), ((), ())), preferred_element_type=F32
            )
            out = out + (ans_c[k] * scale) * piece
        mat_ref[:, part] = out[:own_rows]
    vec = 0.0
    for k in range(ITERS):
        vec = vec + (ans_c[k] * scale) * vecs[k]
    vec_ref[...] = vec


def per_device(spins, energies, counts, accepted, hidden_bias, weights):
    n_chain = lax.axis_size("chain")
    n_rep = lax.axis_size("rep")
    slots, sites = spins.shape
    hidden = weights.shape[1]
    visible = sites // n_rep
    bits = n_chain.bit_length() - 1
    vec_rows = -(-(hidden // LANES + 1) // 8) * 8
    order = jnp.arange(slots, dtype=jnp.int32)
    names = jnp.where(order < counts[0], accepted[0], -1)
    live = jnp.any(order[:, None] == names[None, :], axis=1).astype(F32)
    vmem = pl.BlockSpec(memory_space=pltpu.VMEM)
    dma = pltpu.SemaphoreType.DMA
    mat, vec = pl.pallas_call(
        functools.partial(kernel, n_chain, n_rep),
        out_shape=(
            jax.ShapeDtypeStruct((sites // n_chain, hidden), F32),
            jax.ShapeDtypeStruct((vec_rows, LANES), F32),
        ),
        in_specs=[vmem] * 6,
        out_specs=(vmem, vmem),
        scratch_shapes=[
            pltpu.VMEM((hidden, slots), BF16),
            pltpu.VMEM((hidden, sites), F32),
            pltpu.VMEM((hidden + MIN_ROWS * bits, sites), BF16),
            pltpu.VMEM((hidden + MIN_ROWS * bits, sites), BF16),
            pltpu.VMEM((ITERS, hidden, sites), BF16),
            pltpu.VMEM((ITERS, vec_rows, LANES), F32),
            pltpu.VMEM((ITERS, bits, vec_rows, LANES), F32),
            pltpu.VMEM((8, slots), F32),
            pltpu.VMEM((ITERS, n_rep, 8, slots), F32),
            pltpu.VMEM((ITERS + 1, n_chain, 8, LANES), F32),
            dma((ITERS, bits)),
            dma((ITERS, bits)),
            dma((ITERS, bits)),
            dma((ITERS, bits)),
            dma((ITERS, bits)),
            dma((ITERS, bits)),
            dma((ITERS, n_rep)),
            dma((ITERS, n_rep)),
            dma((ITERS + 1, n_chain)),
            dma((ITERS + 1, n_chain)),
        ],
        compiler_params=pltpu.CompilerParams(
            collective_id=0, has_side_effects=True, vmem_limit_bytes=60 * 1024 * 1024
        ),
    )(
        spins,
        spins.T,
        weights.T,
        hidden_bias.astype(F32).reshape(hidden // LANES, LANES),
        energies.astype(F32)[None],
        live[None],
    )
    flat = vec.reshape(-1)
    return flat[hidden : hidden + visible], flat[:hidden], mat


def solution(mesh):
    in_specs = (
        P("chain", None),
        P("chain"),
        P("chain"),
        P("chain", None),
        P("rep"),
        P(None, "rep"),
    )
    out_specs = (P("rep"), P("rep"), P("chain", "rep"))
    return jax.shard_map(
        per_device, mesh=mesh, in_specs=in_specs, out_specs=out_specs, check_vma=False
    )
```

time: 714 us -> 173 us (0.24); the launches traced: 706 us -> 172 us
  blocking collectives: 288 us -> 0 us
  waiting for transfers between devices: 219 us -> 0 us
  Pallas kernels: 0 us -> 158 us
  matrix products: 88.2 us -> 0 us
  between operations: 44.1 us -> 1.39 us
  other arithmetic: 45.5 us -> 3.21 us
  local copies, waits for them, and re-layouts: 20.7 us -> 9.59 us
    psum x15 -> x0, blocking collectives: 288 us -> none  [the longest x4 126 us: pull(): lax.psum((grad_vis, grad_hid, grad_mat), 'chain')]
    psum x4 -> x0, waiting for transfers between devices: 219 us -> none  [pull(): lax.psum((grad_vis, grad_hid, grad_mat), 'chain')]
    pallas_call x0 -> x1, Pallas kernels: none -> 158 us  [per_device(): pl.pallas_call(functools.partial(kernel, n_chain, n_rep), out_shape=(jax....]
    dot_general x18 -> x0, matrix products: 88.2 us -> none  [the longest x4 40.2 us: pull(): jnp.einsum('ri,rj->ij', samples, weighted, precision=PRECISE, preferred_e...]
    reduce_sum x19 -> x0, other arithmetic: 38.6 us -> none  [the longest x4 18 us: inner(): jnp.sum(first_vec[2] * second_vec[2])]
    gather x2 -> x0, local copies, waits for them, and re-layouts: 14.2 us -> none  [the longest x1 9.46 us: per_device(): energy = energies[accepted_row].astype(jnp.float32)]
  transfers between devices with their start and end apart: 4 -> 0, of which waited for: 4 -> 0; matrix products, arithmetic and copies ran while one was open for 4% -> 0% of each run, Pallas kernels for 0% -> 0%
where the time goes in v2:
time: 173 us; the launch traced here: 172 us
  Pallas kernels  158 us (91%)
  local copies, waits for them, and re-layouts  9.59 us (6%)
  other arithmetic  3.21 us (2%)
    pallas_call x1, Pallas kernels, per_device(): pl.pallas_call(functools.partial(kernel, n_chain, n_rep), out_shape=(jax....  158 us
    unnamed x5, local copies, waits for them, and re-layouts  5.22 us

profile of v2, /device:TPU:0, one launch (start us, length us, event | category | flops | bytes accessed | tf_op | source)
XLA Modules:
  0.0 172.4 jit_solution(1297662364991489341)
XLA Ops:
  0.6 0.0 copy-start
  1.4 1.3 reshape.34.energy_ref
  2.7 0.7 fusion.1
  3.4 1.2 fusion
  4.6 0.6 reshape.35.live_ref
  5.2 1.3 bitcast_convert_fusion.bias_ref
  6.5 2.3 %copy.11 = bf16[1536,256]{0,1:T(8,128)(2,1)} copy(bf16[1536,256]{1,0:T(8,128)(2,1)} %s_ref.1) | data formatting | bytes 1572864 | tf_op args[0]
  8.8 0.0 copy-done
  8.8 1.3 copy.12
  10.1 158.3 %shard_map.85 = (f32[16,2048]{1,0:T(8,128)}, f32[24,128]{1,0:T(8,128)}) custom-call(bf16[1536,256]{1,0:T(8,128)(2,1)} %s_ref.1, bf16[256,1536]{1,0:T(8,128)(2,1)} %bitcast.12, bf16[2048,256]{1,0:T(8,128)(2,1)} %bitcast.11, f32[16,128]{1,0:T(8,128)} %bitcast_convert_fusion.bias_ref, f32[1,1536]{1,0:T(1,128)} %reshape.34.energy_ref, f32[1,1536]{1,0:T(1,128)} %reshape.35.live_ref), custom_call_target="tpu_custom_call" | custom-call | tf_op jit(solution)/shard_map/pallas_call | solution.py:334
  168.4 1.2 slice_bitcast_fusion.1
  169.6 1.3 slice_bitcast_fusion
  170.9 1.6 copy.15
  (1 shorter events, 0.0 us)
Async XLA Ops:
  0.6 8.2 %copy-start = (bf16[256,2048]{1,0:T(8,128)(2,1)S(1)}, bf16[256,2048]{1,0:T(8,128)(2,1)}, u32[]{:S(2)}) copy-start(bf16[256,2048]{1,0:T(8,128)(2,1)} %param.11) | copy-start | bytes 3145732

commit v3 on v2

--- a/solution.py
+++ b/solution.py
@@ -15,6 +15,7 @@
 DIAG_SHIFT = 0.05
 EPSILON = 1e-06
 LANES = 128
+MAX_STRANDS = 4
 MIN_ROWS = 16
 MESH = pl.DeviceIdType.MESH
 F32 = jnp.float32
@@ -27,6 +28,12 @@
 
 def to_column(row):
     return jnp.transpose(jnp.broadcast_to(row, (LANES, LANES)))[:, :1]
+
+
+def bit_order(strand, bits):
+    rest = list(range(1, bits))
+    turn = strand % len(rest)
+    return [0] + rest[turn:] + rest[:turn]
 
 
 def total(values):
@@ -44,7 +51,8 @@
     visible = sites // n_rep
     sample_total = float(KEEP_DEV * n_chain)
     bits = n_chain.bit_length() - 1
-    tile = min(256, hidden // 2)
+    strands = min(MAX_STRANDS, hidden // 256)
+    tile = min(256, hidden // (2 * strands))
     chunks = tile // LANES
     vis_row = hidden // LANES
     me = lax.axis_index("chain")
@@ -164,69 +172,84 @@
             sums = jnp.concatenate([sums, jnp.zeros((LANES - visible, 1), F32)], axis=0)
         vecs[k, vis_row : vis_row + 1, :] = to_row(sums)
 
-        start, size, place = 0, hidden, 0
-        steps = []
-        for b in range(bits):
-            digit, partner = peer(b)
-            split = size // 2 >= MIN_ROWS
-            moved = size // 2 if split else size
-            away = start + (1 - digit) * moved if split else start
-            keep = start + digit * moved if split else start
-            away = pl.multiple_of(away, moved)
-            keep = pl.multiple_of(keep, moved)
-            if b == 0:
-                pull_tiles(k, away, moved // tile, row_weight)
-            outbox[pl.ds(place, moved), :] = acc[pl.ds(away, moved), :].astype(BF16)
-            send = pltpu.make_async_remote_copy(
-                src_ref=outbox.at[pl.ds(place, moved)],
-                dst_ref=inbox.at[pl.ds(place, moved)],
-                send_sem=mat_send.at[k, b],
-                recv_sem=mat_recv.at[k, b],
+        rowsum[...] = jnp.zeros_like(rowsum)
+
+        def mat_copy(source, target, sends, recvs, slot, partner):
+            return pltpu.make_async_remote_copy(
+                src_ref=source,
+                dst_ref=target,
+                send_sem=sends.at[k, slot],
+                recv_sem=recvs.at[k, slot],
                 device_id={"chain": partner},
                 device_id_type=MESH,
             )
-            send.start()
-            if b == 0:
-                pull_tiles(k, keep, moved // tile, row_weight)
-            spread = pltpu.make_async_remote_copy(
-                src_ref=vecs.at[k],
-                dst_ref=vec_in.at[k, b],
-                send_sem=vec_send.at[k, b],
-                recv_sem=vec_recv.at[k, b],
-                device_id={"chain": partner},
-                device_id_type=MESH,
-            )
-            spread.start()
-            send.wait()
-            own = acc[pl.ds(keep, moved), :]
-            if not split:
-                own = own.astype(BF16).astype(F32)
-            acc[pl.ds(keep, moved), :] = own + inbox[pl.ds(place, moved), :].astype(F32)
-            spread.wait()
-            vecs[k] = vecs[k] + vec_in[k, b]
-            place += moved
-            start, size = keep, moved
-            steps.append((b, partner, split, keep, moved))
-        pulled[k, pl.ds(start, size), :] = acc[pl.ds(start, size), :].astype(BF16)
-        rowsum[...] = jnp.zeros_like(rowsum)
-        for b, partner, split, keep, moved in reversed(steps):
-            if not split:
-                continue
-            part = pl.ds(pl.multiple_of(keep, moved), moved)
-            send = pltpu.make_async_remote_copy(
-                src_ref=pulled.at[k, part],
-                dst_ref=pulled.at[k, part],
-                send_sem=back_send.at[k, b],
-                recv_sem=back_recv.at[k, b],
-                device_id={"chain": partner},
-                device_id_type=MESH,
-            )
-            send.start()
-            if b == 0:
-                push_tiles(k, keep, moved // tile)
-            send.wait()
-            if b == 0:
-                push_tiles(k, hidden - moved - keep, moved // tile)
+
+        def strand(c, order):
+            size = hidden // strands
+            start, place = c * size, c * (size + MIN_ROWS * bits)
+            steps = []
+            for b in order:
+                digit, partner = peer(b)
+                split = size // 2 >= MIN_ROWS
+                moved = size // 2 if split else size
+                away = start + (1 - digit) * moved if split else start
+                keep = start + digit * moved if split else start
+                away = pl.multiple_of(away, moved)
+                keep = pl.multiple_of(keep, moved)
+                if b == order[0]:
+                    pull_tiles(k, away, moved // tile, row_weight)
+                outbox[pl.ds(place, moved), :] = acc[pl.ds(away, moved), :].astype(BF16)
+                box = pl.ds(place, moved)
+                send = mat_copy(
+                    outbox.at[box], inbox.at[box], mat_send, mat_recv, c * bits + b, partner
+                )
+                send.start()
+                yield
+                if b == order[0]:
+                    pull_tiles(k, keep, moved // tile, row_weight)
+                send.wait()
+                own = acc[pl.ds(keep, moved), :]
+                if not split:
+                    own = own.astype(BF16).astype(F32)
+                acc[pl.ds(keep, moved), :] = own + inbox[box, :].astype(F32)
+                place += moved
+                start, size = keep, moved
+                steps.append((b, partner, split, keep, moved))
+            pulled[k, pl.ds(start, size), :] = acc[pl.ds(start, size), :].astype(BF16)
+            for b, partner, split, keep, moved in reversed(steps):
+                if not split:
+                    continue
+                part = pulled.at[k, pl.ds(pl.multiple_of(keep, moved), moved)]
+                send = mat_copy(part, part, back_send, back_recv, c * bits + b, partner)
+                send.start()
+                yield
+                if b == order[0]:
+                    push_tiles(k, keep, moved // tile)
+                    yield
+                send.wait()
+                if b == order[0]:
+                    other = 2 * c * (hidden // strands) + hidden // strands - moved - keep
+                    push_tiles(k, other, moved // tile)
+
+        def vec_strand():
+            yield
+            for b in range(bits):
+                spread = pltpu.make_async_remote_copy(
+                    src_ref=vecs.at[k],
+                    dst_ref=vec_in.at[k, b],
+                    send_sem=vec_send.at[k, b],
+                    recv_sem=vec_recv.at[k, b],
+                    device_id={"chain": peer(b)[1]},
+                    device_id_type=MESH,
+                )
+                spread.start()
+                yield
+                spread.wait()
+                vecs[k] = vecs[k] + vec_in[k, b]
+
+        active = [strand(c, bit_order(c, bits)) for c in range(strands)] + [vec_strand()]
+        while active:
+            active = [one for one in active if next(one, active) is not active]
         seen = jnp.sum(rowsum[...], axis=0, keepdims=True)
         effect = to_column(vecs[k, vis_row : vis_row + 1, :])[:visible]
         seen = seen + jnp.sum(st_ref[own_visible, :].astype(F32) * effect, axis=0, keepdims=True)
@@ -325,6 +348,7 @@
     hidden = weights.shape[1]
     visible = sites // n_rep
     bits = n_chain.bit_length() - 1
+    strands = min(MAX_STRANDS, hidden // 256)
     vec_rows = -(-(hidden // LANES + 1) // 8) * 8
     order = jnp.arange(slots, dtype=jnp.int32)
     names = jnp.where(order < counts[0], accepted[0], -1)
@@ -342,18 +366,18 @@
         scratch_shapes=[
             pltpu.VMEM((hidden, slots), BF16),
             pltpu.VMEM((hidden, sites), F32),
-            pltpu.VMEM((hidden + MIN_ROWS * bits, sites), BF16),
-            pltpu.VMEM((hidden + MIN_ROWS * bits, sites), BF16),
+            pltpu.VMEM((hidden + strands * MIN_ROWS * bits, sites), BF16),
+            pltpu.VMEM((hidden + strands * MIN_ROWS * bits, sites), BF16),
             pltpu.VMEM((ITERS, hidden, sites), BF16),
             pltpu.VMEM((ITERS, vec_rows, LANES), F32),
             pltpu.VMEM((ITERS, bits, vec_rows, LANES), F32),
             pltpu.VMEM((8, slots), F32),
             pltpu.VMEM((ITERS, n_rep, 8, slots), F32),
             pltpu.VMEM((ITERS + 1, n_chain, 8, LANES), F32),
-            dma((ITERS, bits)),
-            dma((ITERS, bits)),
-            dma((ITERS, bits)),
-            dma((ITERS, bits)),
+            dma((ITERS, strands * bits)),
+            dma((ITERS, strands * bits)),
+            dma((ITERS, strands * bits)),
+            dma((ITERS, strands * bits)),
             dma((ITERS, bits)),
             dma((ITERS, bits)),
             dma((ITERS, n_rep)),

time: 173 us -> 141 us (0.82)
  Pallas kernels: 158 us -> 127 us
    pallas_call x1, Pallas kernels: 158 us -> 127 us  [per_device(): pl.pallas_call(functools.partial(kernel, n_chain, n_rep), out_shape=(jax....]
where the time goes in v3:
time: 141 us
  Pallas kernels  127 us (90%)
  local copies, waits for them, and re-layouts  9.59 us (7%)
  other arithmetic  3.21 us (2%)
    pallas_call x1, Pallas kernels, per_device(): pl.pallas_call(functools.partial(kernel, n_chain, n_rep), out_shape=(jax....  127 us
    unnamed x5, local copies, waits for them, and re-layouts  5.22 us

profile of v3, /device:TPU:0, one launch (start us, length us, event | category | flops | bytes accessed | tf_op | source)
XLA Modules:
  0.0 140.8 jit_solution(13825026369889687124)
XLA Ops:
  0.6 0.0 copy-start
  1.4 1.3 reshape.34.energy_ref
  2.7 0.7 fusion.1
  3.4 1.2 fusion
  4.6 0.6 reshape.35.live_ref
  5.2 1.3 bitcast_convert_fusion.bias_ref
  6.5 2.3 %copy.11 = bf16[1536,256]{0,1:T(8,128)(2,1)} copy(bf16[1536,256]{1,0:T(8,128)(2,1)} %s_ref.1) | data formatting | bytes 1572864 | tf_op args[0]
  8.8 0.0 copy-done
  8.8 1.3 copy.12
  10.1 126.6 %shard_map.85 = (f32[16,2048]{1,0:T(8,128)}, f32[24,128]{1,0:T(8,128)}) custom-call(bf16[1536,256]{1,0:T(8,128)(2,1)} %s_ref.1, bf16[256,1536]{1,0:T(8,128)(2,1)} %bitcast.12, bf16[2048,256]{1,0:T(8,128)(2,1)} %bitcast.11, f32[16,128]{1,0:T(8,128)} %bitcast_convert_fusion.bias_ref, f32[1,1536]{1,0:T(1,128)} %reshape.34.energy_ref, f32[1,1536]{1,0:T(1,128)} %reshape.35.live_ref), custom_call_target="tpu_custom_call" | custom-call | tf_op jit(solution)/shard_map/pallas_call | solution.py:358
  136.7 1.2 slice_bitcast_fusion.1
  137.9 1.3 slice_bitcast_fusion
  139.2 1.6 %copy.15 = f32[16,2048]{1,0:T(8,128)} copy(f32[16,2048]{1,0:T(8,128)} %get-tuple-element.12) | data formatting | bytes 262144
  (1 shorter events, 0.0 us)
Async XLA Ops:
  0.6 8.2 %copy-start = (bf16[256,2048]{1,0:T(8,128)(2,1)S(1)}, bf16[256,2048]{1,0:T(8,128)(2,1)}, u32[]{:S(2)}) copy-start(bf16[256,2048]{1,0:T(8,128)(2,1)} %param.11) | copy-start | bytes 3145732
